TPU v7x, 32 devices: a whole 2x2x4 slice. The times are simulated.
32 devices in a mesh: seq: 16 (over z, y, core), head: 2 (over x).
Axes of the slice: x: 2, y: 2, z: 4, core: 2. Of those that a mesh axis runs over, the one named last changes fastest.
Arguments:
- queries: bfloat16 [8192, 4096], P('seq', 'head'), may hold values from -20 to 20
- key_rows: bfloat16 [8192, 2048], P('seq', 'head'), may hold values from -20 to 20
- values: bfloat16 [8192, 2048], P('seq', 'head'), may hold values from -24 to 24
- out_weight: bfloat16 [4096, 5376], P('head'), may hold values from -0.09375 to 0.09375
Outputs:
- projected: bfloat16 [8192, 5376], P(('seq', 'head'))
All inputs are finite; a program needn't handle non-finite values.
Results may differ from a plain program's by a relative error of at most 0.019.
Values may be sent and summed in bfloat16 or wider, within the bound.
A program may use at most 192 MiB of HBM per device.

v0:
```python
import jax
import jax.numpy as jnp
from jax import lax
from jax.sharding import PartitionSpec as P

HD = 128
attn_scale = 168.0 ** (-0.5)
neg_fill = -1e30
key_block = 512


def from_behind(value, axis, steps):
    count = lax.axis_size(axis)
    leading, last = (max(0, -steps), min(count, count - steps))
    return lax.ppermute(value, axis, [(source, source + steps) for source in range(leading, last)])


def for_sending(x):

    def short(part):
        return part.astype(jnp.bfloat16) if part.dtype == jnp.float32 else part

    return jax.tree.map(short, x)


def attend(states, query_part, query_begin, key_part, value_part, key_begin, key_low, key_high):
    query_len = query_part.shape[0]
    key_len = key_part.shape[0]
    needed = (
        (key_begin <= query_begin + query_len - 1)
        & (key_begin + key_len > key_low)
        & (key_begin < key_high)
    )

    def compute(states):
        row_max, row_sum, summed = states
        query_pos = query_begin + jnp.arange(query_len, dtype=jnp.int32)
        key_pos = key_begin + jnp.arange(key_len, dtype=jnp.int32)
        allowed = (
            (key_pos[None, :] <= query_pos[:, None])
            & (key_pos[None, :] >= key_low)
            & (key_pos[None, :] < key_high)
        )
        scores = (
            jnp.einsum("qhgd,khd->hgqk", query_part, key_part, preferred_element_type=jnp.float32)
            * attn_scale
        )
        scores = jnp.where(allowed[None, None], scores, neg_fill)
        new_max = jnp.maximum(row_max, jnp.max(scores, axis=-1))
        weights = jnp.where(allowed[None, None], jnp.exp(scores - new_max[..., None]), 0.0)
        factor = jnp.exp(row_max - new_max)
        new_sum = row_sum * factor + jnp.sum(weights, axis=-1)
        rounded = weights.astype(jnp.bfloat16)
        new_summed = summed * factor[..., None] + jnp.einsum(
            "hgqk,khd->hgqd", rounded, value_part, preferred_element_type=jnp.float32
        )
        return (new_max, new_sum, new_summed)

    return lax.cond(needed, compute, lambda kept: kept, states)


def fresh_state(value_heads, per_group, local_rows):
    return (
        jnp.full((value_heads, per_group, local_rows), neg_fill, jnp.float32),
        jnp.zeros((value_heads, per_group, local_rows), jnp.float32),
        jnp.zeros((value_heads, per_group, local_rows, HD), jnp.float32),
    )


def per_device(queries, key_rows, values, out_weight):
    spans = lax.axis_size("seq")
    myself = lax.axis_index("seq")
    local_rows = queries.shape[0]
    value_heads = key_rows.shape[1] // HD
    query_heads = queries.shape[1] // HD
    per_group = query_heads // value_heads
    own_grid = queries.reshape(local_rows, value_heads, per_group, HD)
    own_begin = myself * local_rows
    query_sets = []
    half_axis = spans // 2
    lent_limit = spans // 4 * local_rows
    is_late = myself >= half_axis
    own_low = jnp.where(is_late, lent_limit, 0).astype(jnp.int32)
    query_sets.append((own_grid, own_begin, own_low, jnp.int32(2**30)))
    lent = from_behind(queries, "seq", -half_axis)
    lent_grid = lent.reshape(local_rows, value_heads, per_group, HD)
    lent_high = jnp.where(is_late, 0, lent_limit).astype(jnp.int32)
    query_sets.append((lent_grid, (myself + half_axis) * local_rows, jnp.int32(0), lent_high))
    initial = tuple((fresh_state(value_heads, per_group, local_rows) for entry in query_sets))
    key_piece = lax.all_gather(key_rows, "seq", axis=0, tiled=True)
    value_piece = lax.all_gather(values, "seq", axis=0, tiled=True)
    piece_rows = key_piece.shape[0]
    block_total = piece_rows // key_block

    def advance(block_id, inner):
        key_slab = lax.dynamic_slice_in_dim(key_piece, block_id * key_block, key_block, 0).reshape(
            key_block, value_heads, HD
        )
        value_slab = lax.dynamic_slice_in_dim(
            value_piece, block_id * key_block, key_block, 0
        ).reshape(key_block, value_heads, HD)
        key_begin = block_id * key_block
        return tuple(
            (
                attend(state_one, grid, begin, key_slab, value_slab, key_begin, lower, upper)
                for state_one, (grid, begin, lower, upper) in zip(inner, query_sets)
            )
        )

    results = lax.fori_loop(0, block_total, advance, initial)
    row_max, row_sum, summed = results[0]
    back_max, back_sum, back_summed = from_behind(for_sending(results[1]), "seq", spans // 2)
    back_max = jnp.where(myself >= spans // 2, back_max, neg_fill)
    joint_max = jnp.maximum(row_max, back_max)
    own_factor = jnp.exp(row_max - joint_max)
    back_factor = jnp.exp(back_max - joint_max)
    row_sum = row_sum * own_factor + back_sum * back_factor
    summed = summed * own_factor[..., None] + back_summed * back_factor[..., None]
    attended = (
        (summed / row_sum[..., None])
        .transpose(2, 0, 1, 3)
        .reshape(local_rows, query_heads * HD)
        .astype(jnp.bfloat16)
    )
    return lax.psum_scatter(
        jnp.dot(attended, out_weight, preferred_element_type=jnp.float32).astype(jnp.bfloat16),
        "head",
        scatter_dimension=0,
        tiled=True,
    )


def solution(mesh):
    placed = (P("seq", "head"), P("seq", "head"), P("seq", "head"), P("head", None))
    return jax.shard_map(
        per_device, mesh=mesh, in_specs=placed, out_specs=P(("seq", "head"), None), check_vma=False
    )
```

profile of v0, /device:TPU:0, one launch (start us, length us, event | category | flops | bytes accessed | tf_op | source)
XLA Modules:
  0.0 802.0 jit_solution(6045147930715456967)
XLA Ops:
  11.3 3.9 copy.15
  16.5 3.1 copy.17
  19.6 179.8 %collective-permute-done = bf16[512,2048]{0,1:T(8,128)(2,1)} collective-permute-done((bf16[512,2048]{0,1:T(8,128)(2,1)}, bf16[512,2048]{0,1:T(8,128)(2,1)}, u32[]{:S(2)}, u32[]{:S(2)}) %collective-permute-start) | collective-permute-done | bytes 2097184 | tf_op jit(solution)/shard_map/ppermute | solution.py:15
  199.4 3.9 copy.18
  203.3 14.5 %all-gather.3.cloned.1.call-done = bf16[8192,1024]{0,1:T(8,128)(2,1)} async-done(((bf16[512,1024]{0,1:T(8,128)(2,1)}), bf16[8192,1024]{0,1:T(8,128)(2,1)}) %all-gather.3.cloned.1.call-update) | async-done | bytes 16777232 | tf_op jit(solution)/shard_map/all_gather | solution.py:90
  217.8 133.6 %all-gather.5.cloned.1.call-done = bf16[8192,1024]{0,1:T(8,128)(2,1)} async-done(((bf16[512,1024]{0,1:T(8,128)(2,1)}), bf16[8192,1024]{0,1:T(8,128)(2,1)}) %all-gather.5.cloned.1.call-update) | async-done | bytes 16777232 | tf_op jit(solution)/shard_map/all_gather | solution.py:91
  356.4 161.2 %while.26 = (s32[]{:T(128)}, f32[8,2,512]{2,1,0:T(2,128)S(1)}, f32[8,2,512]{2,1,0:T(2,128)S(1)}, f32[8,2,512,128]{3,2,1,0:T(8,128)}, f32[8,2,512]{2,1,0:T(2,128)...) while((s32[]{:T(128)}, f32[8,2,512]{2,1,0:T(2,128)S(1)}, ...), condition=%wide.region_9.10_spmd, body=%wide.region_0.9_spmd.sunk | while | flops 4409824256 | bytes 342905664 | solution.py:110
  356.4 2.7 constant_dynamic-slice_fusion.3
  359.1 22.8 %conditional.4 = ((f32[8,2,512]{2,1,0:T(2,128)S(1)}, f32[8,2,512]{2,1,0:T(2,128)S(1)}, f32[8,2,512,128]{3,2,1,0:T(8,128)})) conditional(s32[]{:T(128)} %convert_element_type.91, (f32[8,2,512]{2,1,0:T(2,128)S(1)}, f32[8,2,512]{2,1,0:T(2,128)S(1)}, f32[8,2,512,128]{3,2,1,0:T(8,128)}) %tuple.74, (s32[]{:T(128)}, s32[]{:T(128)}, s32[]{:T(128)}, ...), branch_computations={%region_1.1_spmd, %region_2.4_spmd} | conditional | flops 2204912128 | bytes 169355424 | solution.py:59
  359.4 3.8 fusion
  363.2 4.0 fusion.2
  367.2 3.3 copy-done
  370.6 9.2 %multiply_add_fusion = f32[8,2,512,128]{3,2,1,0:T(8,128)S(1)} fusion(f32[8,2,512,128]{3,2,1,0:T(8,128)S(1)} %copy-done.6, f32[8,2,512]{2,1,0:T(2,128)S(1)} %bitcast.92, f32[8,512,512,2]{2,1,3,0:T(8,128)} %copy-done, f32[8,2,512]{2,1,0:T(2,128)S(1)} %max.6, pred[512,512]{0,1:T(8,128)(4,1)S(1)} %and_and_fusion, bf16[512,8,128]{0,2,1:T(8,128)(2,1)S(1)} %copy-done.2), kind=kOutput, calls=%fused_computation.7 | convolution fusion | flops 1096810496 | bytes 26542080 | tf_op jit(solution)/shard_map/while/body/eval_jaxpr/cond/branch_1_fun/hgqk,khd->hgqd/dot_general | solution.py:54
  381.9 24.0 %conditional.5 = ((f32[8,2,512]{2,1,0:T(2,128)S(1)}, f32[8,2,512]{2,1,0:T(2,128)S(1)}, f32[8,2,512,128]{3,2,1,0:T(8,128)})) conditional(s32[]{:T(128)} %convert_element_type.92, (f32[8,2,512]{2,1,0:T(2,128)S(1)}, f32[8,2,512]{2,1,0:T(2,128)S(1)}, f32[8,2,512,128]{3,2,1,0:T(8,128)}) %tuple.76, (s32[]{:T(128)}, s32[]{:T(128)}, s32[]{:T(128)}, ...), branch_computations={%region_5.5_spmd, %region_6.8_spmd} | conditional | flops 2204912128 | bytes 169355424 | solution.py:59
  382.2 5.0 fusion.16
  387.2 4.0 fusion.18
  391.3 3.3 copy-done.1
  394.7 9.2 %multiply_add_fusion.2 = f32[8,2,512,128]{3,2,1,0:T(8,128)S(1)} fusion(f32[8,2,512,128]{3,2,1,0:T(8,128)S(1)} %copy-done.4, f32[8,2,512]{2,1,0:T(2,128)S(1)} %bitcast.93, f32[8,512,512,2]{2,1,3,0:T(8,128)} %copy-done.1, f32[8,2,512]{2,1,0:T(2,128)S(1)} %max.7, pred[512,512]{0,1:T(8,128)(4,1)S(1)} %and_and_fusion.1, bf16[512,8,128]{0,2,1:T(8,128)(2,1)S(1)} %copy-done.3), kind=kOutput, calls=%fused_computation.28 | convolution fusion | flops 1096810496 | bytes 26542080 | tf_op jit(solution)/shard_map/while/body/eval_jaxpr/cond/branch_1_fun/hgqk,khd->hgqd/dot_general | solution.py:54
  405.8 2.7 constant_dynamic-slice_fusion.3
  408.5 24.0 %conditional.5 = ((f32[8,2,512]{2,1,0:T(2,128)S(1)}, f32[8,2,512]{2,1,0:T(2,128)S(1)}, f32[8,2,512,128]{3,2,1,0:T(8,128)})) conditional(s32[]{:T(128)} %convert_element_type.92, (f32[8,2,512]{2,1,0:T(2,128)S(1)}, f32[8,2,512]{2,1,0:T(2,128)S(1)}, f32[8,2,512,128]{3,2,1,0:T(8,128)}) %tuple.76, (s32[]{:T(128)}, s32[]{:T(128)}, s32[]{:T(128)}, ...), branch_computations={%region_5.5_spmd, %region_6.8_spmd} | conditional | flops 2204912128 | bytes 169355424 | solution.py:59
  408.8 5.0 fusion.16
  413.9 4.0 fusion.18
  417.9 3.3 copy-done.1
  421.3 9.2 %multiply_add_fusion.2 = f32[8,2,512,128]{3,2,1,0:T(8,128)S(1)} fusion(f32[8,2,512,128]{3,2,1,0:T(8,128)S(1)} %copy-done.4, f32[8,2,512]{2,1,0:T(2,128)S(1)} %bitcast.93, f32[8,512,512,2]{2,1,3,0:T(8,128)} %copy-done.1, f32[8,2,512]{2,1,0:T(2,128)S(1)} %max.7, pred[512,512]{0,1:T(8,128)(4,1)S(1)} %and_and_fusion.1, bf16[512,8,128]{0,2,1:T(8,128)(2,1)S(1)} %copy-done.3), kind=kOutput, calls=%fused_computation.28 | convolution fusion | flops 1096810496 | bytes 26542080 | tf_op jit(solution)/shard_map/while/body/eval_jaxpr/cond/branch_1_fun/hgqk,khd->hgqd/dot_general | solution.py:54
  432.5 2.7 constant_dynamic-slice_fusion.3
  435.1 24.0 %conditional.5 = ((f32[8,2,512]{2,1,0:T(2,128)S(1)}, f32[8,2,512]{2,1,0:T(2,128)S(1)}, f32[8,2,512,128]{3,2,1,0:T(8,128)})) conditional(s32[]{:T(128)} %convert_element_type.92, (f32[8,2,512]{2,1,0:T(2,128)S(1)}, f32[8,2,512]{2,1,0:T(2,128)S(1)}, f32[8,2,512,128]{3,2,1,0:T(8,128)}) %tuple.76, (s32[]{:T(128)}, s32[]{:T(128)}, s32[]{:T(128)}, ...), branch_computations={%region_5.5_spmd, %region_6.8_spmd} | conditional | flops 2204912128 | bytes 169355424 | solution.py:59
  435.4 5.0 fusion.16
  440.5 4.0 fusion.18
  444.5 3.3 copy-done.1
  447.9 9.2 %multiply_add_fusion.2 = f32[8,2,512,128]{3,2,1,0:T(8,128)S(1)} fusion(f32[8,2,512,128]{3,2,1,0:T(8,128)S(1)} %copy-done.4, f32[8,2,512]{2,1,0:T(2,128)S(1)} %bitcast.93, f32[8,512,512,2]{2,1,3,0:T(8,128)} %copy-done.1, f32[8,2,512]{2,1,0:T(2,128)S(1)} %max.7, pred[512,512]{0,1:T(8,128)(4,1)S(1)} %and_and_fusion.1, bf16[512,8,128]{0,2,1:T(8,128)(2,1)S(1)} %copy-done.3), kind=kOutput, calls=%fused_computation.28 | convolution fusion | flops 1096810496 | bytes 26542080 | tf_op jit(solution)/shard_map/while/body/eval_jaxpr/cond/branch_1_fun/hgqk,khd->hgqd/dot_general | solution.py:54
  459.1 2.7 constant_dynamic-slice_fusion.3
  461.8 24.0 %conditional.5 = ((f32[8,2,512]{2,1,0:T(2,128)S(1)}, f32[8,2,512]{2,1,0:T(2,128)S(1)}, f32[8,2,512,128]{3,2,1,0:T(8,128)})) conditional(s32[]{:T(128)} %convert_element_type.92, (f32[8,2,512]{2,1,0:T(2,128)S(1)}, f32[8,2,512]{2,1,0:T(2,128)S(1)}, f32[8,2,512,128]{3,2,1,0:T(8,128)}) %tuple.76, (s32[]{:T(128)}, s32[]{:T(128)}, s32[]{:T(128)}, ...), branch_computations={%region_5.5_spmd, %region_6.8_spmd} | conditional | flops 2204912128 | bytes 169355424 | solution.py:59
  462.1 5.0 fusion.16
  467.1 4.0 fusion.18
  471.2 3.3 copy-done.1
  474.6 9.2 %multiply_add_fusion.2 = f32[8,2,512,128]{3,2,1,0:T(8,128)S(1)} fusion(f32[8,2,512,128]{3,2,1,0:T(8,128)S(1)} %copy-done.4, f32[8,2,512]{2,1,0:T(2,128)S(1)} %bitcast.93, f32[8,512,512,2]{2,1,3,0:T(8,128)} %copy-done.1, f32[8,2,512]{2,1,0:T(2,128)S(1)} %max.7, pred[512,512]{0,1:T(8,128)(4,1)S(1)} %and_and_fusion.1, bf16[512,8,128]{0,2,1:T(8,128)(2,1)S(1)} %copy-done.3), kind=kOutput, calls=%fused_computation.28 | convolution fusion | flops 1096810496 | bytes 26542080 | tf_op jit(solution)/shard_map/while/body/eval_jaxpr/cond/branch_1_fun/hgqk,khd->hgqd/dot_general | solution.py:54
  485.7 2.7 constant_dynamic-slice_fusion.3
  488.4 2.7 constant_dynamic-slice_fusion.3
  491.0 2.7 constant_dynamic-slice_fusion.3
  493.7 2.7 constant_dynamic-slice_fusion.3
  499.0 2.7 constant_dynamic-slice_fusion.3
  501.7 2.7 constant_dynamic-slice_fusion.3
  517.6 3.3 copy.20
  526.4 5.3 copy.19
  531.8 14.5 %collective-permute-done.3 = bf16[8,2,512]{2,1,0:T(2,128)(2,1)S(1)} collective-permute-done((bf16[8,2,512]{2,1,0:T(2,128)(2,1)S(1)}, bf16[8,2,512]{2,1,0:T(2,128)(2,1)S(1)}, u32[]{:S(2)}, u32[]{:S(2)}) %collective-permute-start.3) | collective-permute-done | bytes 16416 | tf_op jit(solution)/shard_map/ppermute | solution.py:15
  546.7 3.7 divide_convert_fusion
  550.5 18.6 %convolution_convert_fusion = bf16[512,5376]{1,0:T(8,128)(2,1)} fusion(bf16[512,2048]{0,1:T(8,128)(2,1)S(1)} %bitcast.87, bf16[2048,5376]{1,0:T(8,128)(2,1)} %param.13), kind=kOutput, calls=%fused_computation.44 | convolution fusion | flops 11277041664 | bytes 29622272 | tf_op jit(solution)/shard_map/dot_general | solution.py:126
  569.0 226.5 %reduce-scatter.2.cloned.1.call-done = bf16[256,5376]{1,0:T(8,128)(2,1)} async-done(((bf16[512,5376]{1,0:T(8,128)(2,1)}), bf16[256,5376]{1,0:T(8,128)(2,1)}) %reduce-scatter.2.cloned.1.call-update) | async-done | bytes 2752528 | tf_op jit(solution)/shard_map/reduce_scatter | solution.py:125
  (121 shorter events, 44.5 us)
Async XLA Ops:
  6.5 211.2 %all-gather.3.cloned.1.call-start = ((), (), s32[]{:S(2)}) async-start(), calls=%async_computation.1 | async-start | bytes 17825792 | tf_op jit(solution)/shard_map/all_gather | solution.py:90
  8.8 342.5 %all-gather.5.cloned.1.call-start = ((), (), s32[]{:S(2)}) async-start(), calls=%async_computation.2 | async-start | bytes 17825792 | tf_op jit(solution)/shard_map/all_gather | solution.py:91
  11.2 784.3 %reduce-scatter.2.cloned.1.call-start = ((), (), s32[]{:S(2)}) async-start(), calls=%async_computation.3 | async-start | bytes 8257536 | tf_op jit(solution)/shard_map/reduce_scatter | solution.py:125
  15.2 184.2 %collective-permute-start = (bf16[512,2048]{0,1:T(8,128)(2,1)}, bf16[512,2048]{0,1:T(8,128)(2,1)}, u32[]{:S(2)}, u32[]{:S(2)}) collective-permute-start(bf16[512,2048]{0,1:T(8,128)(2,1)} %copy.15), channel_id=1, source_target_pairs={{16,0},{18,2},{20,4},{22,6},{24,8},{26,10},{28,12},{30,14},{17,1},... | collective-permute-start | bytes 6291464 | tf_op jit(solution)/shard_map/ppermute | solution.py:15
  363.1 7.4 copy-start
  363.2 7.4 copy-start.2
  363.2 7.4 copy-start.6
  379.8 2.1 copy-start.7
  387.2 7.4 copy-start.1
  387.2 7.4 copy-start.3
  387.2 7.4 copy-start.4
  403.8 2.0 copy-start.5
  413.8 7.4 copy-start.1
  413.8 7.4 copy-start.3
  413.8 7.4 copy-start.4
  430.5 2.0 copy-start.5
  440.4 7.4 copy-start.1
  440.5 7.4 copy-start.3
  440.5 7.4 copy-start.4
  457.1 2.0 copy-start.5
  467.1 7.4 copy-start.1
  467.1 7.4 copy-start.3
  467.1 7.4 copy-start.4
  483.7 2.0 copy-start.5
  521.0 25.7 %collective-permute-start.2 = (bf16[8,2,512,128]{2,3,1,0:T(8,128)(2,1)S(1)}, bf16[8,2,512,128]{2,3,1,0:T(8,128)(2,1)}, u32[]{:S(2)}, u32[]{:S(2)}) collective-permute-start(bf16[8,2,512,128]{2,3,1,0:T(8,128)(2,1)S(1)} %copy.20), channel_id=1, source_target_pairs={{0,16},{2,18},{4,20},{6,22},{8,24},{10,26},{12,28},{14,30},{1,17},... | collective-permute-start | bytes 6291464 | tf_op jit(solution)/shard_map/ppermute | solution.py:15
  523.6 22.6 %collective-permute-start.3 = (bf16[8,2,512]{2,1,0:T(2,128)(2,1)S(1)}, bf16[8,2,512]{2,1,0:T(2,128)(2,1)S(1)}, u32[]{:S(2)}, u32[]{:S(2)}) collective-permute-start(bf16[8,2,512]{2,1,0:T(2,128)(2,1)S(1)} %convert_element_type.63), channel_id=1, source_target_pairs={{0,16},{2,18},{4,20},{6,22},{8,24},{10,26},{12,28},{14,30},{1,17},... | collective-permute-start | bytes 49160 | tf_op jit(solution)/shard_map/ppermute | solution.py:15
  525.1 21.5 %collective-permute-start.1 = (bf16[8,2,512]{2,1,0:T(2,128)(2,1)S(1)}, bf16[8,2,512]{2,1,0:T(2,128)(2,1)S(1)}, u32[]{:S(2)}, u32[]{:S(2)}) collective-permute-start(bf16[8,2,512]{2,1,0:T(2,128)(2,1)S(1)} %convert_element_type.59), channel_id=1, source_target_pairs={{0,16},{2,18},{4,20},{6,22},{8,24},{10,26},{12,28},{14,30},{1,17},... | collective-permute-start | bytes 49160 | tf_op jit(solution)/shard_map/ppermute | solution.py:15
Sparse Core Ops, SparseCore 0:
  9.5 208.2 all-gather.2
  219.9 131.4 all-gather.4
  569.1 226.2 reduce-scatter.1
where the time goes:
time: 804 us; the launch traced here: 802 us
  waiting for transfers between devices  569 us (71%)
  local copies, waits for them, and re-layouts  98.4 us (12%)
  matrix products  88.1 us (11%)
  other arithmetic  25.7 us (3%)
  between operations  13.2 us (2%)
    reduce_scatter x1, waiting for transfers between devices, per_device(): lax.psum_scatter(jnp.dot(attended, out_weight, preferred_element_type=jnp...  226 us
    ppermute x4, waiting for transfers between devices, from_behind(): lax.ppermute(value, axis, [(source, source + steps) for source in range(l...  195 us
    all_gather x1, waiting for transfers between devices, per_device(): value_piece = lax.all_gather(values, 'seq', axis=0, tiled=True)  134 us
    dot_general x5, matrix products, compute(): jnp.einsum('hgqk,khd->hgqd', rounded, value_part, preferred_element_type=...  45.8 us
    dynamic_slice x16, local copies, waits for them, and re-layouts, advance(): lax.dynamic_slice_in_dim(value_piece, block_id * key_block, key_block, 0)  42.5 us
    cond x45, local copies, waits for them, and re-layouts  26.8 us
    dot_general x5, matrix products, compute(): jnp.einsum('qhgd,khd->hgqk', query_part, key_part, preferred_element_type...  23.7 us
    reduce_sum x5, other arithmetic, compute(): new_sum = row_sum * factor + jnp.sum(weights, axis=-1)  20.2 us
  transfers between devices with their start and end apart: 7, of which 6 were waited for; matrix products, arithmetic and copies ran while one was open for 2% of the time, Pallas kernels for 0%

commit v1 on v0

--- a/solution.py
+++ b/solution.py
@@ -88,7 +88,9 @@
     query_sets.append((lent_grid, (myself + half_axis) * local_rows, jnp.int32(0), lent_high))
     initial = tuple((fresh_state(value_heads, per_group, local_rows) for entry in query_sets))
     key_piece = lax.all_gather(key_rows, "seq", axis=0, tiled=True)
-    value_piece = lax.all_gather(values, "seq", axis=0, tiled=True)
+    value_piece = jnp.concatenate(
+        lax.all_to_all(jnp.stack([values] * lax.axis_size("seq")), "seq", 0, 0), axis=0
+    )
     piece_rows = key_piece.shape[0]
     block_total = piece_rows // key_block
 

time: 804 us -> 1080 us (1.34)
  waiting for transfers between devices: 569 us -> 768 us
  local copies, waits for them, and re-layouts: 98.4 us -> 164 us
    ppermute x4, waiting for transfers between devices: 195 us -> 561 us  [from_behind(): lax.ppermute(value, axis, [(source, source + steps) for source in range(l...]
    all_gather x1 -> x0, waiting for transfers between devices: 134 us -> none  [per_device(): value_piece = lax.all_gather(values, 'seq', axis=0, tiled=True)]
    all_to_all x0 -> x1, local copies, waits for them, and re-layouts: none -> 21.7 us  [per_device(): lax.all_to_all(jnp.stack([values] * lax.axis_size('seq')), 'seq', 0, 0)]
    dynamic_slice x0 -> x16, local copies, waits for them, and re-layouts: none -> 20.7 us  [advance(): lax.dynamic_slice_in_dim(key_piece, block_id * key_block, key_block, 0)]
    cond x45, local copies, waits for them, and re-layouts: 26.8 us -> 47 us
    reduce_scatter x1, waiting for transfers between devices: 226 us -> 208 us  [per_device(): lax.psum_scatter(jnp.dot(attended, out_weight, preferred_element_type=jnp...]
    all_gather x1, waiting for transfers between devices: 14.5 us -> 0.01 us  [per_device(): key_piece = lax.all_gather(key_rows, 'seq', axis=0, tiled=True)]
    dynamic_slice x16 -> x32, local copies, waits for them, and re-layouts: 42.5 us -> 42.1 us  [advance(): lax.dynamic_slice_in_dim(value_piece, block_id * key_block, key_block, 0)]
  transfers between devices with their start and end apart: 7 -> 7, of which waited for: 6 -> 4; matrix products, arithmetic and copies ran while one was open for 2% -> 4% of each run, Pallas kernels for 0% -> 0%
where the time goes in v1:
time: 1080 us
  waiting for transfers between devices  768 us (71%)
  local copies, waits for them, and re-layouts  164 us (15%)
  matrix products  88.1 us (8%)
  other arithmetic  25.7 us (2%)
  starting transfers between devices  14.3 us (1%)
  between operations  13.6 us (1%)
    ppermute x4, waiting for transfers between devices, from_behind(): lax.ppermute(value, axis, [(source, source + steps) for source in range(l...  561 us
    reduce_scatter x1, waiting for transfers between devices, per_device(): lax.psum_scatter(jnp.dot(attended, out_weight, preferred_element_type=jnp...  208 us
    cond x45, local copies, waits for them, and re-layouts  47 us
    dot_general x5, matrix products, compute(): jnp.einsum('hgqk,khd->hgqd', rounded, value_part, preferred_element_type=...  45.8 us
    dynamic_slice x32, local copies, waits for them, and re-layouts, advance(): lax.dynamic_slice_in_dim(value_piece, block_id * key_block, key_block, 0)  42.1 us
    dot_general x5, matrix products, compute(): jnp.einsum('qhgd,khd->hgqk', query_part, key_part, preferred_element_type...  23.7 us
    all_to_all x1, local copies, waits for them, and re-layouts, per_device(): lax.all_to_all(jnp.stack([values] * lax.axis_size('seq')), 'seq', 0, 0)  21.7 us
  transfers between devices with their start and end apart: 7, of which 4 were waited for; matrix products, arithmetic and copies ran while one was open for 4% of the time, Pallas kernels for 0%

profile of v1, /device:TPU:0, one launch (start us, length us, event | category | flops | bytes accessed | tf_op | source)
XLA Modules:
  0.0 1075.6 jit_solution(11821352901738687113)
XLA Ops:
  6.5 1.5 copy.42
  8.0 5.9 stack.2
  14.0 7.7 all-to-all-start
  23.2 2.5 copy.44
  27.0 3.0 copy.47
  30.1 546.3 %collective-permute-done = bf16[512,2048]{0,1:T(8,128)(2,1)} collective-permute-done((bf16[512,2048]{0,1:T(8,128)(2,1)}, bf16[512,2048]{0,1:T(8,128)(2,1)}, u32[]{:S(2)}, u32[]{:S(2)}) %collective-permute-start) | collective-permute-done | bytes 2097184 | tf_op jit(solution)/shard_map/ppermute | solution.py:15
  576.4 3.9 copy.48
  580.3 21.7 %copy.43 = bf16[16,512,1024]{2,1,0:T(8,128)(2,1)} copy(bf16[16,512,1024]{1,2,0:T(8,128)(2,1)} %all-to-all-done) | data formatting | bytes 33554432 | tf_op jit(solution)/shard_map/all_to_all | solution.py:92
  602.0 2.4 broadcast.164.clone
  604.5 2.5 broadcast.164
  607.0 203.2 %while.26 = (s32[]{:T(128)}, f32[8,2,512]{2,1,0:T(2,128)S(1)}, f32[8,2,512]{2,1,0:T(2,128)S(1)}, f32[8,2,512,128]{3,2,1,0:T(8,128)}, f32[8,2,512]{2,1,0:T(2,128)...) while((s32[]{:T(128)}, f32[8,2,512]{2,1,0:T(2,128)S(1)}, ...), condition=%wide.region_9.10_spmd, body=%wide.region_0.9_spmd.sunk | while | flops 4409824256 | bytes 345002816 | solution.py:112
  610.9 26.9 %conditional.4 = ((f32[8,2,512]{2,1,0:T(2,128)S(1)}, f32[8,2,512]{2,1,0:T(2,128)S(1)}, f32[8,2,512,128]{3,2,1,0:T(8,128)})) conditional(s32[]{:T(128)} %convert_element_type.91, (f32[8,2,512]{2,1,0:T(2,128)S(1)}, f32[8,2,512]{2,1,0:T(2,128)S(1)}, f32[8,2,512,128]{3,2,1,0:T(8,128)}) %tuple.77, (s32[]{:T(128)}, s32[]{:T(128)}, s32[]{:T(128)}, ...), branch_computations={%region_1.1_spmd, %region_2.4_spmd} | conditional | flops 2204912128 | bytes 169355424 | solution.py:59
  611.2 3.7 fusion
  615.1 7.4 copy-done
  622.4 4.0 fusion.2
  626.5 9.2 multiply_add_fusion
  635.7 2.1 copy-done.7
  637.8 28.0 %conditional.5 = ((f32[8,2,512]{2,1,0:T(2,128)S(1)}, f32[8,2,512]{2,1,0:T(2,128)S(1)}, f32[8,2,512,128]{3,2,1,0:T(8,128)})) conditional(s32[]{:T(128)} %convert_element_type.92, (f32[8,2,512]{2,1,0:T(2,128)S(1)}, f32[8,2,512]{2,1,0:T(2,128)S(1)}, f32[8,2,512,128]{3,2,1,0:T(8,128)}) %tuple.79, (s32[]{:T(128)}, s32[]{:T(128)}, s32[]{:T(128)}, ...), branch_computations={%region_5.5_spmd, %region_6.8_spmd} | conditional | flops 2204912128 | bytes 169355424 | solution.py:59
  638.1 5.0 fusion.16
  643.1 7.4 copy-done.1
  650.5 4.0 fusion.18
  654.6 9.2 multiply_add_fusion.2
  663.8 2.0 copy-done.5
  669.7 28.0 %conditional.5 = ((f32[8,2,512]{2,1,0:T(2,128)S(1)}, f32[8,2,512]{2,1,0:T(2,128)S(1)}, f32[8,2,512,128]{3,2,1,0:T(8,128)})) conditional(s32[]{:T(128)} %convert_element_type.92, (f32[8,2,512]{2,1,0:T(2,128)S(1)}, f32[8,2,512]{2,1,0:T(2,128)S(1)}, f32[8,2,512,128]{3,2,1,0:T(8,128)}) %tuple.79, (s32[]{:T(128)}, s32[]{:T(128)}, s32[]{:T(128)}, ...), branch_computations={%region_5.5_spmd, %region_6.8_spmd} | conditional | flops 2204912128 | bytes 169355424 | solution.py:59
  670.1 5.0 fusion.16
  675.1 7.4 copy-done.1
  682.5 4.0 fusion.18
  686.6 9.2 multiply_add_fusion.2
  695.8 2.0 copy-done.5
  701.7 28.0 %conditional.5 = ((f32[8,2,512]{2,1,0:T(2,128)S(1)}, f32[8,2,512]{2,1,0:T(2,128)S(1)}, f32[8,2,512,128]{3,2,1,0:T(8,128)})) conditional(s32[]{:T(128)} %convert_element_type.92, (f32[8,2,512]{2,1,0:T(2,128)S(1)}, f32[8,2,512]{2,1,0:T(2,128)S(1)}, f32[8,2,512,128]{3,2,1,0:T(8,128)}) %tuple.79, (s32[]{:T(128)}, s32[]{:T(128)}, s32[]{:T(128)}, ...), branch_computations={%region_5.5_spmd, %region_6.8_spmd} | conditional | flops 2204912128 | bytes 169355424 | solution.py:59
  702.1 5.0 fusion.16
  707.1 7.4 copy-done.1
  714.5 4.0 fusion.18
  718.6 9.2 multiply_add_fusion.2
  727.8 2.0 copy-done.5
  733.7 28.0 %conditional.5 = ((f32[8,2,512]{2,1,0:T(2,128)S(1)}, f32[8,2,512]{2,1,0:T(2,128)S(1)}, f32[8,2,512,128]{3,2,1,0:T(8,128)})) conditional(s32[]{:T(128)} %convert_element_type.92, (f32[8,2,512]{2,1,0:T(2,128)S(1)}, f32[8,2,512]{2,1,0:T(2,128)S(1)}, f32[8,2,512,128]{3,2,1,0:T(8,128)}) %tuple.79, (s32[]{:T(128)}, s32[]{:T(128)}, s32[]{:T(128)}, ...), branch_computations={%region_5.5_spmd, %region_6.8_spmd} | conditional | flops 2204912128 | bytes 169355424 | solution.py:59
  734.1 5.0 fusion.16
  739.1 7.4 copy-done.1
  746.5 4.0 fusion.18
  750.6 9.2 multiply_add_fusion.2
  759.8 2.0 copy-done.5
  810.2 3.4 copy.50
  813.6 2.6 collective-permute-start.2
  818.8 5.6 copy.49
  824.4 14.2 %collective-permute-done.3 = bf16[8,2,512]{2,1,0:T(2,128)(2,1)S(1)} collective-permute-done((bf16[8,2,512]{2,1,0:T(2,128)(2,1)S(1)}, bf16[8,2,512]{2,1,0:T(2,128)(2,1)S(1)}, u32[]{:S(2)}, u32[]{:S(2)}) %collective-permute-start.3) | collective-permute-done | bytes 16416 | tf_op jit(solution)/shard_map/ppermute | solution.py:15
  838.8 3.7 divide_convert_fusion
  842.6 18.6 %convolution_convert_fusion = bf16[512,5376]{1,0:T(8,128)(2,1)} fusion(bf16[512,2048]{0,1:T(8,128)(2,1)S(1)} %bitcast.89, bf16[2048,5376]{1,0:T(8,128)(2,1)} %param.13), kind=kOutput, calls=%fused_computation.44 | convolution fusion | flops 11277041664 | bytes 29622272 | tf_op jit(solution)/shard_map/dot_general | solution.py:128
  861.2 207.6 %reduce-scatter.2.cloned.1.call-done = bf16[256,5376]{1,0:T(8,128)(2,1)} async-done(((bf16[512,5376]{1,0:T(8,128)(2,1)}), bf16[256,5376]{1,0:T(8,128)(2,1)}) %reduce-scatter.2.cloned.1.call-update) | async-done | bytes 2752528 | tf_op jit(solution)/shard_map/reduce_scatter | solution.py:127
  (158 shorter events, 70.7 us)
Async XLA Ops:
  14.0 7.8 copy-start.9
  14.0 9.2 copy-start.8
  14.0 566.3 %all-to-all-start = ((bf16[16,512,1024]{1,2,0:T(8,128)(2,1)}), bf16[16,512,1024]{1,2,0:T(8,128)(2,1)}, u32[]{:S(2)}, u32[]{:S(2)}) async-start(bf16[16,512,1024]{1,2,0:T(8,128)(2,1)} %stack.2), calls=%async_computation | async-start | bytes 33554432 | tf_op jit(solution)/shard_map/all_to_all | solution.py:92
  21.7 580.2 %all-gather.2.cloned.1.call-start = ((), (), s32[]{:S(2)}) async-start(), calls=%async_computation.2 | async-start | bytes 17825792 | tf_op jit(solution)/shard_map/all_gather | solution.py:90
  23.2 1045.6 %reduce-scatter.2.cloned.1.call-start = ((), (), s32[]{:S(2)}) async-start(), calls=%async_computation.3 | async-start | bytes 8257536 | tf_op jit(solution)/shard_map/reduce_scatter | solution.py:127
  25.7 550.7 %collective-permute-start = (bf16[512,2048]{0,1:T(8,128)(2,1)}, bf16[512,2048]{0,1:T(8,128)(2,1)}, u32[]{:S(2)}, u32[]{:S(2)}) collective-permute-start(bf16[512,2048]{0,1:T(8,128)(2,1)} %copy.44), channel_id=1, source_target_pairs={{16,0},{18,2},{20,4},{22,6},{24,8},{26,10},{28,12},{30,14},{17,1},... | collective-permute-start | bytes 6291464 | tf_op jit(solution)/shard_map/ppermute | solution.py:15
  615.0 7.4 copy-start
  615.0 11.5 %copy-start.2 = (bf16[512,8,128]{0,2,1:T(8,128)(2,1)S(1)}, bf16[512,8,128]{0,2,1:T(8,128)(2,1)}, u32[]{:S(2)}) copy-start(bf16[512,8,128]{0,2,1:T(8,128)(2,1)} %get-tuple-element.591) | copy-start | bytes 3145732 | tf_op jit(solution)/shard_map/while/body/eval_jaxpr/cond
  615.0 11.5 %copy-start.6 = (f32[8,2,512,128]{3,2,1,0:T(8,128)S(1)}, f32[8,2,512,128]{3,2,1,0:T(8,128)}, u32[]{:S(2)}) copy-start(f32[8,2,512,128]{3,2,1,0:T(8,128)} %get-tuple-element.466) | copy-start | bytes 12582916 | tf_op jit(solution)/shard_map/while/body/eval_jaxpr/cond
  635.7 2.1 copy-start.7
  643.1 7.4 copy-start.1
  643.1 11.5 %copy-start.3 = (bf16[512,8,128]{0,2,1:T(8,128)(2,1)S(1)}, bf16[512,8,128]{0,2,1:T(8,128)(2,1)}, u32[]{:S(2)}) copy-start(bf16[512,8,128]{0,2,1:T(8,128)(2,1)} %get-tuple-element.600) | copy-start | bytes 3145732 | tf_op jit(solution)/shard_map/while/body/eval_jaxpr/cond
  643.1 11.5 %copy-start.4 = (f32[8,2,512,128]{3,2,1,0:T(8,128)S(1)}, f32[8,2,512,128]{3,2,1,0:T(8,128)}, u32[]{:S(2)}) copy-start(f32[8,2,512,128]{3,2,1,0:T(8,128)} %get-tuple-element.475) | copy-start | bytes 12582916 | tf_op jit(solution)/shard_map/while/body/eval_jaxpr/cond
  663.8 2.0 copy-start.5
  675.1 7.4 copy-start.1
  675.1 11.5 %copy-start.3 = (bf16[512,8,128]{0,2,1:T(8,128)(2,1)S(1)}, bf16[512,8,128]{0,2,1:T(8,128)(2,1)}, u32[]{:S(2)}) copy-start(bf16[512,8,128]{0,2,1:T(8,128)(2,1)} %get-tuple-element.600) | copy-start | bytes 3145732 | tf_op jit(solution)/shard_map/while/body/eval_jaxpr/cond
  675.1 11.5 %copy-start.4 = (f32[8,2,512,128]{3,2,1,0:T(8,128)S(1)}, f32[8,2,512,128]{3,2,1,0:T(8,128)}, u32[]{:S(2)}) copy-start(f32[8,2,512,128]{3,2,1,0:T(8,128)} %get-tuple-element.475) | copy-start | bytes 12582916 | tf_op jit(solution)/shard_map/while/body/eval_jaxpr/cond
  695.8 2.0 copy-start.5
  707.1 7.4 copy-start.1
  707.1 11.5 %copy-start.3 = (bf16[512,8,128]{0,2,1:T(8,128)(2,1)S(1)}, bf16[512,8,128]{0,2,1:T(8,128)(2,1)}, u32[]{:S(2)}) copy-start(bf16[512,8,128]{0,2,1:T(8,128)(2,1)} %get-tuple-element.600) | copy-start | bytes 3145732 | tf_op jit(solution)/shard_map/while/body/eval_jaxpr/cond
  707.1 11.5 %copy-start.4 = (f32[8,2,512,128]{3,2,1,0:T(8,128)S(1)}, f32[8,2,512,128]{3,2,1,0:T(8,128)}, u32[]{:S(2)}) copy-start(f32[8,2,512,128]{3,2,1,0:T(8,128)} %get-tuple-element.475) | copy-start | bytes 12582916 | tf_op jit(solution)/shard_map/while/body/eval_jaxpr/cond
  727.8 2.0 copy-start.5
  739.1 7.4 copy-start.1
  739.1 11.5 %copy-start.3 = (bf16[512,8,128]{0,2,1:T(8,128)(2,1)S(1)}, bf16[512,8,128]{0,2,1:T(8,128)(2,1)}, u32[]{:S(2)}) copy-start(bf16[512,8,128]{0,2,1:T(8,128)(2,1)} %get-tuple-element.600) | copy-start | bytes 3145732 | tf_op jit(solution)/shard_map/while/body/eval_jaxpr/cond
  739.1 11.5 %copy-start.4 = (f32[8,2,512,128]{3,2,1,0:T(8,128)S(1)}, f32[8,2,512,128]{3,2,1,0:T(8,128)}, u32[]{:S(2)}) copy-start(f32[8,2,512,128]{3,2,1,0:T(8,128)} %get-tuple-element.475) | copy-start | bytes 12582916 | tf_op jit(solution)/shard_map/while/body/eval_jaxpr/cond
  759.8 2.0 copy-start.5
  813.6 25.3 %collective-permute-start.2 = (bf16[8,2,512,128]{2,3,1,0:T(8,128)(2,1)S(1)}, bf16[8,2,512,128]{2,3,1,0:T(8,128)(2,1)}, u32[]{:S(2)}, u32[]{:S(2)}) collective-permute-start(bf16[8,2,512,128]{2,3,1,0:T(8,128)(2,1)S(1)} %copy.50), channel_id=1, source_target_pairs={{0,16},{2,18},{4,20},{6,22},{8,24},{10,26},{12,28},{14,30},{1,17},... | collective-permute-start | bytes 6291464 | tf_op jit(solution)/shard_map/ppermute | solution.py:15
  816.2 22.3 %collective-permute-start.3 = (bf16[8,2,512]{2,1,0:T(2,128)(2,1)S(1)}, bf16[8,2,512]{2,1,0:T(2,128)(2,1)S(1)}, u32[]{:S(2)}, u32[]{:S(2)}) collective-permute-start(bf16[8,2,512]{2,1,0:T(2,128)(2,1)S(1)} %convert_element_type.63), channel_id=1, source_target_pairs={{0,16},{2,18},{4,20},{6,22},{8,24},{10,26},{12,28},{14,30},{1,17},... | collective-permute-start | bytes 49160 | tf_op jit(solution)/shard_map/ppermute | solution.py:15
  817.5 21.2 %collective-permute-start.1 = (bf16[8,2,512]{2,1,0:T(2,128)(2,1)S(1)}, bf16[8,2,512]{2,1,0:T(2,128)(2,1)S(1)}, u32[]{:S(2)}, u32[]{:S(2)}) collective-permute-start(bf16[8,2,512]{2,1,0:T(2,128)(2,1)S(1)} %convert_element_type.59), channel_id=1, source_target_pairs={{0,16},{2,18},{4,20},{6,22},{8,24},{10,26},{12,28},{14,30},{1,17},... | collective-permute-start | bytes 49160 | tf_op jit(solution)/shard_map/ppermute | solution.py:15
Sparse Core Ops, SparseCore 0:
  24.7 369.0 all-gather.1
  861.3 207.3 reduce-scatter.1
